TPU v7x, 256 devices: a whole 4x4x8 slice. The times are simulated.
256 devices in a mesh: layer: 4 (over y), front: 64 (over z, x, core).
Axes of the slice: x: 4, y: 4, z: 8, core: 2. Of those that a mesh axis runs over, the one named last changes fastest.
Arguments:
- right_sides: float32 [4, 2, 4, 8192], P('layer', None, None, 'front'), may hold values from -6 to 6
- leaf_inverse: bfloat16 [4, 2, 8192, 128], P('layer', None, 'front'), may hold values from -0.375 to 0.375
- couple_above: bfloat16 [4, 2, 8192, 128], P('layer', None, 'front'), may hold values from -0.1875 to 0.1875
- couple_below: bfloat16 [4, 2, 8192, 128], P('layer', None, 'front'), may hold values from -0.1875 to 0.1875
- sep_gather: bfloat16 [4, 2, 5120, 8192], P('layer', None, None, 'front'), may hold values from -0.046875 to 0.046875
- sep_inverse: bfloat16 [4, 2, 5120, 5120], P('layer', None, 'front'), may hold values from -0.0625 to 0.0625
- sep_spread: bfloat16 [4, 2, 8192, 5120], P('layer', None, 'front'), may hold values from -0.0625 to 0.0625
- panel_owner: int32 [4, 64], P('layer'), may hold values from 0 to 63, each once within a row
Outputs:
- solution: float32 [4, 2, 4, 8192], P('layer', None, None, 'front')
Inputs may be any that keep to these rules, and one draw needn't show every extreme that they name: Each row of panel_owner names every slot 0 to 63 once.
All inputs are finite; a program needn't handle non-finite values.
Results may differ from a plain program's by a relative error of at most 0.023.
Values may be sent and summed in bfloat16 or wider, within the bound.
A program may use at most 128 MiB of HBM per device.

v0:
```python
import jax
import jax.numpy as jnp
from jax import lax
from jax.sharding import PartitionSpec as P


def from_behind(block, axis, distance):
    devices = range(lax.axis_size(axis))
    route = [(i - distance, i) for i in devices if i - distance in devices]
    return lax.ppermute(block, axis, route)


def dense_apply(matrix, vector):

    def single(left, right):
        return jnp.dot(right, left.T, preferred_element_type=jnp.float32)

    real_part = single(matrix[0], vector[0]) - single(matrix[1], vector[1])
    imag_part = single(matrix[0], vector[1]) + single(matrix[1], vector[0])
    return jnp.stack([real_part, imag_part])


def layer_solve(source, leaf, gather_map, sep_panel, spread, owner_row):
    leaf_values = dense_apply(leaf, source.astype(jnp.bfloat16))
    partial_sums = dense_apply(gather_map, leaf_values.astype(jnp.bfloat16))
    sep_rounded = lax.psum(partial_sums, "front").astype(jnp.bfloat16)
    own_rows = dense_apply(sep_panel, sep_rounded).astype(jnp.bfloat16)
    stored = lax.all_gather(own_rows, "front", axis=2, tiled=True)
    count = stored.shape[1]
    panels = stored.reshape(2, count, owner_row.shape[0], own_rows.shape[2])
    sep_values = jnp.take(panels, owner_row, axis=2).reshape(2, count, stored.shape[2])
    return leaf_values - dense_apply(spread, sep_values)


def local(
    right_sides,
    leaf_inverse,
    couple_above,
    couple_below,
    sep_gather,
    sep_inverse,
    sep_spread,
    panel_owner,
):
    depth = lax.axis_size("layer")
    owner_row = panel_owner[0]
    sources = right_sides[0]

    def solve(source):
        return layer_solve(
            source, leaf_inverse[0], sep_gather[0], sep_inverse[0], sep_spread[0], owner_row
        )

    forward = solve(sources)
    for step_index in range(depth - 1):
        from_prev = from_behind(forward.astype(jnp.bfloat16), "layer", 1)
        forward = solve(sources - dense_apply(couple_above[0], from_prev))
    solution = forward
    for step_index in range(depth - 1):
        from_next = from_behind(solution.astype(jnp.bfloat16), "layer", -1)
        solution = forward - solve(dense_apply(couple_below[0], from_next))
    return solution[None]


def solution(mesh):
    return jax.shard_map(
        local,
        mesh=mesh,
        in_specs=(
            P("layer", None, None, "front"),
            P("layer", None, "front", None),
            P("layer", None, "front", None),
            P("layer", None, "front", None),
            P("layer", None, None, "front"),
            P("layer", None, "front", None),
            P("layer", None, "front", None),
            P("layer", None),
        ),
        out_specs=P("layer", None, None, "front"),
        check_vma=False,
    )
```

profile of v0, /device:TPU:1, one launch (start us, length us, event | category | flops | bytes accessed | tf_op | source)
XLA Modules:
  0.0 2287.0 jit_solution(15067838010511855414)
XLA Ops:
  10.3 249.5 %all-reduce.7 = bf16[2,4,5120]{2,1,0:T(4,128)(2,1)S(1)} all-reduce(f32[2,4,5120]{2,1,0:T(4,128)S(1)} %pad_maximum_fusion), channel_id=1, replica_groups=mesh['layer'=4,'front'=64] {'front'}, use_global_device_ids=true, to_apply=%region_0.0 | all-reduce | flops 40960 | bytes 245760 | tf_op jit(solution)/shard_map/psum | solution.py:26
  263.7 58.7 %all_gather.21 = bf16[2,4,5120]{1,0,2:T(2,128)(2,1)} all-gather(bf16[2,4,80]{1,0,2:T(2,128)(2,1)S(1)} %copy.58), channel_id=1, replica_groups=mesh['layer'=4,'front'=64] {'front'}, dimensions={2}, use_global_device_ids=true | all-gather | bytes 83200 | tf_op jit(solution)/shard_map/all_gather | solution.py:28
  322.4 5.4 copy.60
  340.8 243.3 %all-reduce.8 = bf16[2,4,5120]{2,1,0:T(4,128)(2,1)S(1)} all-reduce(f32[2,4,5120]{2,1,0:T(4,128)S(1)} %pad_maximum_fusion.1), channel_id=1, replica_groups=mesh['layer'=4,'front'=64] {'front'}, use_global_device_ids=true, to_apply=%region_1.0 | all-reduce | flops 40960 | bytes 245760 | tf_op jit(solution)/shard_map/psum | solution.py:26
  588.0 59.3 %all_gather.22 = bf16[2,4,5120]{1,0,2:T(2,128)(2,1)} all-gather(bf16[2,4,80]{1,0,2:T(2,128)(2,1)S(1)} %copy.63), channel_id=1, replica_groups=mesh['layer'=4,'front'=64] {'front'}, dimensions={2}, use_global_device_ids=true | all-gather | bytes 83200 | tf_op jit(solution)/shard_map/all_gather | solution.py:28
  647.2 5.4 copy.65
  659.8 3.6 collective-permute-start.1
  667.2 243.3 %all-reduce.9 = bf16[2,4,5120]{2,1,0:T(4,128)(2,1)S(1)} all-reduce(f32[2,4,5120]{2,1,0:T(4,128)S(1)} %pad_maximum_fusion.2), channel_id=1, replica_groups=mesh['layer'=4,'front'=64] {'front'}, use_global_device_ids=true, to_apply=%region_2.4 | all-reduce | flops 40960 | bytes 245760 | tf_op jit(solution)/shard_map/psum | solution.py:26
  914.4 58.7 %all_gather.23 = bf16[2,4,5120]{1,0,2:T(2,128)(2,1)} all-gather(bf16[2,4,80]{1,0,2:T(2,128)(2,1)S(1)} %copy.68), channel_id=1, replica_groups=mesh['layer'=4,'front'=64] {'front'}, dimensions={2}, use_global_device_ids=true | all-gather | bytes 83200 | tf_op jit(solution)/shard_map/all_gather | solution.py:28
  973.1 5.4 copy.70
  985.7 3.6 collective-permute-start.2
  993.1 243.5 %all-reduce.10 = bf16[2,4,5120]{2,1,0:T(4,128)(2,1)S(1)} all-reduce(f32[2,4,5120]{2,1,0:T(4,128)S(1)} %pad_maximum_fusion.3), channel_id=1, replica_groups=mesh['layer'=4,'front'=64] {'front'}, use_global_device_ids=true, to_apply=%region_3.5 | all-reduce | flops 40960 | bytes 245760 | tf_op jit(solution)/shard_map/psum | solution.py:26
  1240.5 58.7 %all_gather.24 = bf16[2,4,5120]{1,0,2:T(2,128)(2,1)} all-gather(bf16[2,4,80]{1,0,2:T(2,128)(2,1)S(1)} %copy.73), channel_id=1, replica_groups=mesh['layer'=4,'front'=64] {'front'}, dimensions={2}, use_global_device_ids=true | all-gather | bytes 83200 | tf_op jit(solution)/shard_map/all_gather | solution.py:28
  1299.2 5.4 copy.75
  1313.2 3.3 collective-permute-done.3
  1319.5 243.3 %all-reduce.11 = bf16[2,4,5120]{2,1,0:T(4,128)(2,1)S(1)} all-reduce(f32[2,4,5120]{2,1,0:T(4,128)S(1)} %pad_maximum_fusion.4), channel_id=1, replica_groups=mesh['layer'=4,'front'=64] {'front'}, use_global_device_ids=true, to_apply=%region_4.6 | all-reduce | flops 40960 | bytes 245760 | tf_op jit(solution)/shard_map/psum | solution.py:26
  1566.7 58.7 %all_gather.25 = bf16[2,4,5120]{1,0,2:T(2,128)(2,1)} all-gather(bf16[2,4,80]{1,0,2:T(2,128)(2,1)S(1)} %copy.78), channel_id=1, replica_groups=mesh['layer'=4,'front'=64] {'front'}, dimensions={2}, use_global_device_ids=true | all-gather | bytes 83200 | tf_op jit(solution)/shard_map/all_gather | solution.py:28
  1625.4 5.4 copy.80
  1645.4 243.3 %all-reduce.12 = bf16[2,4,5120]{2,1,0:T(4,128)(2,1)S(1)} all-reduce(f32[2,4,5120]{2,1,0:T(4,128)S(1)} %pad_maximum_fusion.5), channel_id=1, replica_groups=mesh['layer'=4,'front'=64] {'front'}, use_global_device_ids=true, to_apply=%region_5.7 | all-reduce | flops 40960 | bytes 245760 | tf_op jit(solution)/shard_map/psum | solution.py:26
  1892.6 58.7 %all_gather.26 = bf16[2,4,5120]{1,0,2:T(2,128)(2,1)} all-gather(bf16[2,4,80]{1,0,2:T(2,128)(2,1)S(1)} %copy.83), channel_id=1, replica_groups=mesh['layer'=4,'front'=64] {'front'}, dimensions={2}, use_global_device_ids=true | all-gather | bytes 83200 | tf_op jit(solution)/shard_map/all_gather | solution.py:28
  1951.3 5.4 copy.85
  1971.3 243.4 %all-reduce.13 = bf16[2,4,5120]{2,1,0:T(4,128)(2,1)S(1)} all-reduce(f32[2,4,5120]{2,1,0:T(4,128)S(1)} %pad_maximum_fusion.6), channel_id=1, replica_groups=mesh['layer'=4,'front'=64] {'front'}, use_global_device_ids=true, to_apply=%region_6.8 | all-reduce | flops 40960 | bytes 245760 | tf_op jit(solution)/shard_map/psum | solution.py:26
  2218.5 59.0 %all_gather.27 = bf16[2,4,5120]{1,0,2:T(2,128)(2,1)} all-gather(bf16[2,4,80]{1,0,2:T(2,128)(2,1)S(1)} %copy.88), channel_id=1, replica_groups=mesh['layer'=4,'front'=64] {'front'}, dimensions={2}, use_global_device_ids=true | all-gather | bytes 83200 | tf_op jit(solution)/shard_map/all_gather | solution.py:28
  2277.5 5.5 copy.90
  (273 shorter events, 116.2 us)
Async XLA Ops:
  0.0 9.3 copy-start
  259.8 3.1 copy-start.12
  329.1 3.7 copy-start.1
  332.8 4.9 copy-start.9
  332.8 5.4 copy-start.11
  332.8 5.5 copy-start.8
  333.7 3.9 collective-permute-start
  584.1 3.1 copy-start.13
  655.6 3.7 copy-start.2
  659.8 4.3 collective-permute-start.1
  910.5 3.1 copy-start.14
  981.6 3.7 copy-start.3
  985.7 4.3 collective-permute-start.2
  1236.6 3.1 copy-start.15
  1307.7 3.7 copy-start.4
  1309.6 6.9 copy-start.10
  1311.9 4.6 collective-permute-start.3
  1562.8 3.1 copy-start.16
  1633.9 3.7 copy-start.5
  1638.0 4.3 collective-permute-start.4
  1959.8 3.7 copy-start.6
  1964.0 4.3 collective-permute-start.5
  1971.3 246.4 %copy-start.18 = (bf16[1,2,80,5120]{3,2,1,0:T(8,128)(2,1)S(1)}, bf16[1,2,80,5120]{3,2,1,0:T(8,128)(2,1)}, u32[]{:S(2)}) copy-start(bf16[1,2,80,5120]{3,2,1,0:T(8,128)(2,1)} %param.15) | copy-start | bytes 4915204
  2277.5 6.7 copy-start.7
  (1 other events, 3.1 us)
where the time goes:
time: 2300 us; the launch traced here: 2290 us
  blocking collectives  2120 us (92%)
  matrix products  87.5 us (4%)
  local copies, waits for them, and re-layouts  46.7 us (2%)
    psum x7, blocking collectives, layer_solve(): sep_rounded = lax.psum(partial_sums, 'front').astype(jnp.bfloat16)  1710 us
    all_gather x7, blocking collectives, layer_solve(): stored = lax.all_gather(own_rows, 'front', axis=2, tiled=True)  412 us
    dot_general x136, matrix products, single(): return jnp.dot(right, left.T, preferred_element_type=jnp.float32)  87.5 us
  transfers between devices with their start and end apart: 6, of which 6 were waited for; matrix products, arithmetic and copies ran while one was open for 0% of the time, Pallas kernels for 0%

commit v1 on v0

--- a/solution.py
+++ b/solution.py
@@ -25,7 +25,12 @@
     partial_sums = dense_apply(gather_map, leaf_values.astype(jnp.bfloat16))
     sep_rounded = lax.psum(partial_sums, "front").astype(jnp.bfloat16)
     own_rows = dense_apply(sep_panel, sep_rounded).astype(jnp.bfloat16)
-    stored = lax.all_gather(own_rows, "front", axis=2, tiled=True)
+    stored = jnp.concatenate(
+        jax.lax.all_to_all(
+            jnp.stack([own_rows] * jax.lax.axis_size("front"), axis=0), "front", 0, 0
+        ),
+        axis=2,
+    )
     count = stored.shape[1]
     panels = stored.reshape(2, count, owner_row.shape[0], own_rows.shape[2])
     sep_values = jnp.take(panels, owner_row, axis=2).reshape(2, count, stored.shape[2])

time: 2300 us -> 1980 us (0.86)
  blocking collectives: 2120 us -> 1830 us
  local copies, waits for them, and re-layouts: 46.7 us -> 9.15 us
    all_gather x7 -> x0, blocking collectives: 412 us -> none  [layer_solve(): stored = lax.all_gather(own_rows, 'front', axis=2, tiled=True)]
    all_to_all x0 -> x6, blocking collectives: none -> 125 us  [layer_solve(): jax.lax.all_to_all(jnp.stack([own_rows] * jax.lax.axis_size('front'), axi...]
    reshape x7 -> x0, local copies, waits for them, and re-layouts: 37.8 us -> none  [layer_solve(): panels = stored.reshape(2, count, owner_row.shape[0], own_rows.shape[2])]
  transfers between devices with their start and end apart: 6 -> 7, of which waited for: 6 -> 7; matrix products, arithmetic and copies ran while one was open for 0% -> 0% of each run, Pallas kernels for 0% -> 0%
where the time goes in v1:
time: 1980 us
  blocking collectives  1830 us (92%)
  matrix products  90 us (5%)
  starting transfers between devices  24.2 us (1%)
  waiting for transfers between devices  22.6 us (1%)
    psum x7, blocking collectives, layer_solve(): sep_rounded = lax.psum(partial_sums, 'front').astype(jnp.bfloat16)  1700 us
    all_to_all x6, blocking collectives, layer_solve(): jax.lax.all_to_all(jnp.stack([own_rows] * jax.lax.axis_size('front'), axi...  125 us
    dot_general x136, matrix products, single(): return jnp.dot(right, left.T, preferred_element_type=jnp.float32)  90 us
  transfers between devices with their start and end apart: 7, of which 7 were waited for; matrix products, arithmetic and copies ran while one was open for 0% of the time, Pallas kernels for 0%

profile of v1, /device:TPU:1, one launch (start us, length us, event | category | flops | bytes accessed | tf_op | source)
XLA Modules:
  0.0 1976.5 jit_solution(1031925313824171566)
XLA Ops:
  9.0 249.5 %all-reduce.7 = bf16[2,4,5120]{2,1,0:T(4,128)(2,1)S(1)} all-reduce(f32[2,4,5120]{2,1,0:T(4,128)S(1)} %pad_maximum_fusion), channel_id=1, replica_groups=mesh['layer'=4,'front'=64] {'front'}, use_global_device_ids=true, to_apply=%region_0.0 | all-reduce | flops 40960 | bytes 245760 | tf_op jit(solution)/shard_map/psum | solution.py:26
  263.0 9.7 all-to-all-start
  272.7 11.3 all-to-all-done
  290.0 3.2 collective-permute-start
  297.0 241.9 %all-reduce.8 = bf16[2,4,5120]{2,1,0:T(4,128)(2,1)S(1)} all-reduce(f32[2,4,5120]{2,1,0:T(4,128)S(1)} %pad_maximum_fusion.1), channel_id=1, replica_groups=mesh['layer'=4,'front'=64] {'front'}, use_global_device_ids=true, to_apply=%region_1.0 | all-reduce | flops 40960 | bytes 245760 | tf_op jit(solution)/shard_map/psum | solution.py:26
  542.7 20.8 %all_to_all.35 = bf16[64,2,4,80]{3,2,1,0:T(4,128)(2,1)S(1)} all-to-all(bf16[64,2,4,80]{3,2,1,0:T(4,128)(2,1)S(1)} %stack.249), channel_id=1, replica_groups=mesh['layer'=4,'front'=64] {'front'}, dimensions={0} | all-to-all | bytes 163840 | tf_op jit(solution)/shard_map/all_to_all | solution.py:29
  566.5 1.9 fusion.34
  570.7 3.6 collective-permute-start.1
  578.1 242.0 %all-reduce.9 = bf16[2,4,5120]{2,1,0:T(4,128)(2,1)S(1)} all-reduce(f32[2,4,5120]{2,1,0:T(4,128)S(1)} %pad_maximum_fusion.2), channel_id=1, replica_groups=mesh['layer'=4,'front'=64] {'front'}, use_global_device_ids=true, to_apply=%region_2.4 | all-reduce | flops 40960 | bytes 245760 | tf_op jit(solution)/shard_map/psum | solution.py:26
  823.9 20.9 %all_to_all.36 = bf16[64,2,4,80]{3,2,1,0:T(4,128)(2,1)S(1)} all-to-all(bf16[64,2,4,80]{3,2,1,0:T(4,128)(2,1)S(1)} %stack.265), channel_id=1, replica_groups=mesh['layer'=4,'front'=64] {'front'}, dimensions={0} | all-to-all | bytes 163840 | tf_op jit(solution)/shard_map/all_to_all | solution.py:29
  847.9 1.9 fusion.30
  852.0 3.6 collective-permute-start.2
  859.5 242.0 %all-reduce.10 = bf16[2,4,5120]{2,1,0:T(4,128)(2,1)S(1)} all-reduce(f32[2,4,5120]{2,1,0:T(4,128)S(1)} %pad_maximum_fusion.3), channel_id=1, replica_groups=mesh['layer'=4,'front'=64] {'front'}, use_global_device_ids=true, to_apply=%region_3.5 | all-reduce | flops 40960 | bytes 245760 | tf_op jit(solution)/shard_map/psum | solution.py:26
  1105.2 20.9 %all_to_all.37 = bf16[64,2,4,80]{3,2,1,0:T(4,128)(2,1)S(1)} all-to-all(bf16[64,2,4,80]{3,2,1,0:T(4,128)(2,1)S(1)} %stack.284), channel_id=1, replica_groups=mesh['layer'=4,'front'=64] {'front'}, dimensions={0} | all-to-all | bytes 163840 | tf_op jit(solution)/shard_map/all_to_all | solution.py:29
  1134.7 3.3 collective-permute-done.3
  1141.1 242.0 %all-reduce.11 = bf16[2,4,5120]{2,1,0:T(4,128)(2,1)S(1)} all-reduce(f32[2,4,5120]{2,1,0:T(4,128)S(1)} %pad_maximum_fusion.4), channel_id=1, replica_groups=mesh['layer'=4,'front'=64] {'front'}, use_global_device_ids=true, to_apply=%region_4.6 | all-reduce | flops 40960 | bytes 245760 | tf_op jit(solution)/shard_map/psum | solution.py:26
  1386.9 20.9 %all_to_all.38 = bf16[64,2,4,80]{3,2,1,0:T(4,128)(2,1)S(1)} all-to-all(bf16[64,2,4,80]{3,2,1,0:T(4,128)(2,1)S(1)} %stack.300), channel_id=1, replica_groups=mesh['layer'=4,'front'=64] {'front'}, dimensions={0} | all-to-all | bytes 163840 | tf_op jit(solution)/shard_map/all_to_all | solution.py:29
  1416.6 2.8 collective-permute-done.4
  1422.4 242.1 %all-reduce.12 = bf16[2,4,5120]{2,1,0:T(4,128)(2,1)S(1)} all-reduce(f32[2,4,5120]{2,1,0:T(4,128)S(1)} %pad_maximum_fusion.5), channel_id=1, replica_groups=mesh['layer'=4,'front'=64] {'front'}, use_global_device_ids=true, to_apply=%region_5.7 | all-reduce | flops 40960 | bytes 245760 | tf_op jit(solution)/shard_map/psum | solution.py:26
  1668.4 20.8 %all_to_all.39 = bf16[64,2,4,80]{3,2,1,0:T(4,128)(2,1)S(1)} all-to-all(bf16[64,2,4,80]{3,2,1,0:T(4,128)(2,1)S(1)} %stack.313), channel_id=1, replica_groups=mesh['layer'=4,'front'=64] {'front'}, dimensions={0} | all-to-all | bytes 163840 | tf_op jit(solution)/shard_map/all_to_all | solution.py:29
  1692.2 1.9 fusion.18
  1697.7 3.0 collective-permute-done.5
  1703.8 242.1 %all-reduce.13 = bf16[2,4,5120]{2,1,0:T(4,128)(2,1)S(1)} all-reduce(f32[2,4,5120]{2,1,0:T(4,128)S(1)} %pad_maximum_fusion.6), channel_id=1, replica_groups=mesh['layer'=4,'front'=64] {'front'}, use_global_device_ids=true, to_apply=%region_6.8 | all-reduce | flops 40960 | bytes 245760 | tf_op jit(solution)/shard_map/psum | solution.py:26
  1952.0 20.8 %all_to_all.40 = bf16[64,2,4,80]{3,2,1,0:T(4,128)(2,1)S(1)} all-to-all(bf16[64,2,4,80]{3,2,1,0:T(4,128)(2,1)S(1)} %stack.326), channel_id=1, replica_groups=mesh['layer'=4,'front'=64] {'front'}, dimensions={0} | all-to-all | bytes 163840 | tf_op jit(solution)/shard_map/all_to_all | solution.py:29
  (274 shorter events, 102.9 us)
Async XLA Ops:
  0.0 8.0 copy-start
  258.5 3.1 copy-start.12
  260.1 12.6 copy-start.18
  263.0 21.0 %all-to-all-start = ((bf16[64,2,4,80]{3,2,1,0:T(4,128)(2,1)}), bf16[64,2,4,80]{3,2,1,0:T(4,128)(2,1)S(1)}, u32[]{:S(2)}, u32[]{:S(2)}) async-start(bf16[64,2,4,80]{3,2,1,0:T(4,128)(2,1)} %stack.233), calls=%async_computation | async-start | bytes 262144 | tf_op jit(solution)/shard_map/all_to_all | solution.py:29
  285.3 3.7 copy-start.1
  289.0 4.9 copy-start.9
  289.0 5.4 copy-start.11
  289.0 5.5 copy-start.8
  290.0 3.9 collective-permute-start
  538.9 3.1 copy-start.13
  566.5 3.7 copy-start.2
  570.7 4.3 collective-permute-start.1
  847.9 3.7 copy-start.3
  852.0 4.3 collective-permute-start.2
  1129.2 3.7 copy-start.4
  1131.2 6.9 copy-start.10
  1133.4 4.6 collective-permute-start.3
  1383.1 3.1 copy-start.16
  1410.9 3.7 copy-start.5
  1415.0 4.3 collective-permute-start.4
  1664.6 3.1 copy-start.17
  1692.2 3.7 copy-start.6
  1696.4 4.3 collective-permute-start.5
  1948.8 25.1 %copy-start.7 = (bf16[1,2,128,5120]{3,2,1,0:T(8,128)(2,1)S(1)}, bf16[1,2,128,5120]{3,2,1,0:T(8,128)(2,1)}, u32[]{:S(2)}) copy-start(bf16[1,2,128,5120]{3,2,1,0:T(8,128)(2,1)} %param.16) | copy-start | bytes 7864324
  (2 other events, 6.1 us)
